TPU v7x, 512 devices: a whole 4x4x16 slice. The times are simulated.
512 devices in a mesh: gy: 32 (over z, core), gx: 16 (over x, y).
Axes of the slice: x: 4, y: 4, z: 16, core: 2. Of those that a mesh axis runs over, the one named last changes fastest.
Arguments:
- level_in: bfloat16 [256, 1024, 128], P('gy', 'gx'), may hold values from -6 to 6
- w_level: bfloat16 [3, 3, 128, 128], replicated, may hold values from -0.1875 to 0.1875
- w_down: bfloat16 [2, 2, 128, 256], replicated, may hold values from -0.25 to 0.25
- w_neck: bfloat16 [3, 3, 256, 256], replicated, may hold values from -0.125 to 0.125
- cotangent: bfloat16 [128, 512, 256], P('gy', None, 'gx'), may hold values from -6 to 6
Outputs:
- neck_out: bfloat16 [128, 512, 256], P('gy', None, 'gx')
- grad_input: bfloat16 [256, 1024, 128], P('gy', 'gx')
- grad_level: bfloat16 [3, 3, 128, 128], replicated
- grad_down: bfloat16 [2, 2, 128, 256], replicated
- grad_neck: bfloat16 [3, 3, 256, 256], replicated
All inputs are finite; a program needn't handle non-finite values.
Results may differ from a plain program's by a relative error of at most 0.012.
Values may be sent and summed in bfloat16 or wider, within the bound.
A program may use at most 64 MiB of HBM per device.

v0:
```python
import math
import jax
import jax.numpy as jnp
from jax import lax
from jax.sharding import PartitionSpec as P


def extended(cells, sides, width):
    for axis, dim in sides:
        count = lax.axis_size(axis)
        ends = count - 1
        head = lax.slice_in_dim(cells, 0, width, axis=dim)
        tail = lax.slice_in_dim(cells, cells.shape[dim] - width, cells.shape[dim], axis=dim)
        cells = jnp.concatenate(
            [
                lax.ppermute(tail, axis, [(i, (i + 1) % count) for i in range(ends)]),
                cells,
                lax.ppermute(head, axis, [((i + 1) % count, i) for i in range(ends)]),
            ],
            axis=dim,
        )
    return cells


def slope_of(value):
    gate = jax.nn.sigmoid(value)
    return gate + value * gate * (1.0 - gate)


def tile_rims(field_in):
    return extended(field_in, (("gy", 0), ("gx", 1)), 1)


def conv_padded(padded, weights):
    row_count = padded.shape[0] - 2
    col_count = padded.shape[1] - 2
    result = jnp.zeros((row_count * col_count, weights.shape[3]), jnp.float32)
    for offset_y in range(3):
        for offset_x in range(3):
            window = padded[offset_y : offset_y + row_count, offset_x : offset_x + col_count]
            window = window.reshape(row_count * col_count, padded.shape[2])
            result = result + jnp.dot(
                window, weights[offset_y, offset_x], preferred_element_type=jnp.float32
            )
    return result


def weight_terms(padded, grads):
    row_count = grads.shape[0]
    col_count = grads.shape[1]
    flat_grads = grads.reshape(row_count * col_count, grads.shape[2])
    kernel_rows = []
    for offset_y in range(3):
        kernel_row = []
        for offset_x in range(3):
            window = padded[offset_y : offset_y + row_count, offset_x : offset_x + col_count]
            window = window.reshape(row_count * col_count, padded.shape[2])
            kernel_row.append(
                lax.dot_general(
                    window, flat_grads, (((0,), (0,)), ((), ())), preferred_element_type=jnp.float32
                )
            )
        kernel_rows.append(jnp.stack(kernel_row))
    return jnp.stack(kernel_rows)


def local(level_in, w_level, w_down, w_neck, cotangent):
    tile_rows = level_in.shape[0]
    tile_cols = level_in.shape[1]
    level_width = level_in.shape[2]
    neck_width = w_neck.shape[3]
    half_rows = tile_rows // 2
    half_cols = tile_cols // 2
    level_pad = tile_rims(level_in)
    level_pre = conv_padded(level_pad, w_level)
    level_flat = level_in.reshape(tile_rows * tile_cols, level_width).astype(jnp.float32)
    level_act = (level_flat + jax.nn.silu(level_pre)).astype(jnp.bfloat16)
    level_grid = level_act.reshape(half_rows, 2, half_cols, 2, level_width)
    neck_in = jnp.einsum(
        "hpwqc,pqcd->hwd", level_grid, w_down, preferred_element_type=jnp.float32
    ).astype(jnp.bfloat16)
    neck_pad = tile_rims(neck_in)
    neck_pre = conv_padded(neck_pad, w_neck)
    neck_flat = neck_in.reshape(half_rows * half_cols, neck_width).astype(jnp.float32)
    neck_tile = (
        (neck_flat + jax.nn.silu(neck_pre))
        .astype(jnp.bfloat16)
        .reshape(half_rows, half_cols, neck_width)
    )
    neck_out = lax.all_to_all(neck_tile, "gx", split_axis=2, concat_axis=1, tiled=True)
    neck_cot = lax.all_to_all(cotangent, "gx", split_axis=1, concat_axis=2, tiled=True)
    cot_flat = neck_cot.reshape(half_rows * half_cols, neck_width).astype(jnp.float32)
    neck_gate = (
        (cot_flat * slope_of(neck_pre))
        .astype(jnp.bfloat16)
        .reshape(half_rows, half_cols, neck_width)
    )
    flip_neck = jnp.transpose(w_neck[::-1, ::-1], (0, 1, 3, 2))
    gate_pad = tile_rims(neck_gate)
    neck_back = conv_padded(gate_pad, flip_neck)
    cot_tile = neck_cot.reshape(half_rows * half_cols, neck_width).astype(jnp.float32)
    neck_grad = (
        (cot_tile + neck_back).astype(jnp.bfloat16).reshape(half_rows, half_cols, neck_width)
    )
    neck_wgrad = weight_terms(neck_pad, neck_gate)
    level_back = jnp.einsum(
        "hwd,pqcd->hpwqc", neck_grad, w_down, preferred_element_type=jnp.float32
    )
    level_back = level_back.reshape(tile_rows * tile_cols, level_width)
    down_wgrad = jnp.einsum(
        "hpwqc,hwd->pqcd", level_grid, neck_grad, preferred_element_type=jnp.float32
    )
    level_gate = (
        (level_back * slope_of(level_pre))
        .astype(jnp.bfloat16)
        .reshape(tile_rows, tile_cols, level_width)
    )
    flip_level = jnp.transpose(w_level[::-1, ::-1], (0, 1, 3, 2))
    level_gpad = tile_rims(level_gate)
    grad_input = (level_back + conv_padded(level_gpad, flip_level)).astype(jnp.bfloat16)
    grad_input = grad_input.reshape(tile_rows, tile_cols, level_width)
    level_wgrad = weight_terms(level_pad, level_gate)
    device_count = lax.axis_size("gy") * lax.axis_size("gx")
    level_count = tile_rows * tile_cols * device_count
    level_scale = 1.0 / math.sqrt(level_count)
    neck_scale = 1.0 / math.sqrt(level_count // 4)
    reduced = lax.psum((level_wgrad, down_wgrad, neck_wgrad), ("gy", "gx"))
    grad_level = (reduced[0] * level_scale).astype(jnp.bfloat16)
    grad_down = (reduced[1] * neck_scale).astype(jnp.bfloat16)
    grad_neck = (reduced[2] * neck_scale).astype(jnp.bfloat16)
    return (neck_out, grad_input, grad_level, grad_down, grad_neck)


def solution(mesh):
    return jax.shard_map(
        local,
        mesh=mesh,
        in_specs=(P("gy", "gx", None), P(), P(), P(), P("gy", None, "gx")),
        out_specs=(P("gy", None, "gx"), P("gy", "gx", None), P(), P(), P()),
        check_vma=False,
    )
```

profile of v0, /device:TPU:2, one launch (start us, length us, event | category | flops | bytes accessed | tf_op | source)
XLA Modules:
  0.0 618.8 jit_solution(6595421685957169687)
XLA Ops:
  9.7 9.2 %all-to-all-start.1 = ((bf16[16,2,1024]{2,1,0:T(2,128)(2,1)}), bf16[16,2,1024]{2,1,0:T(2,128)(2,1)S(1)}, u32[]{:S(2)}, u32[]{:S(2)}) async-start(bf16[16,2,1024]{2,1,0:T(2,128)(2,1)} %reshape.213), calls=%async_computation.1 | async-start | bytes 131072 | tf_op jit(solution)/shard_map/all_to_all | solution.py:91
  20.2 1.4 collective-permute-start.1
  21.8 2.1 collective-permute-done.1
  24.0 3.4 collective-permute-start.2
  27.4 4.6 collective-permute-start.3
  36.5 1.3 collective-permute-start.5
  37.8 3.9 collective-permute-start.4
  42.5 2.7 collective-permute-start.6
  45.2 5.3 collective-permute-start.7
  55.6 1.4 copy.38
  59.6 1.9 multiply_convert_fusion.4
  68.8 8.5 %all-to-all-start = ((bf16[16,2,1024]{2,1,0:T(2,128)(2,1)}), bf16[16,2,1024]{2,1,0:T(2,128)(2,1)S(1)}, u32[]{:S(2)}, u32[]{:S(2)}) async-start(bf16[16,2,1024]{2,1,0:T(2,128)(2,1)} %reshape.211), calls=%async_computation | async-start | bytes 131072 | tf_op jit(solution)/shard_map/all_to_all | solution.py:90
  77.3 1.3 collective-permute-start.9
  78.7 3.0 collective-permute-start.8
  82.9 1.5 pad_maximum_fusion
  84.5 3.4 collective-permute-start.10
  87.9 4.6 collective-permute-start.11
  98.4 1.3 collective-permute-start.13
  99.7 5.1 collective-permute-start.12
  106.9 2.8 collective-permute-start.14
  109.7 5.3 collective-permute-start.15
  119.9 486.5 %all-reduce.3.cloned.1.call-done = (f32[3,3,128,128]{3,2,1,0:T(8,128)}, f32[2,2,128,256]{3,2,1,0:T(8,128)}, f32[3,3,256,256]{3,2,1,0:T(8,128)}) async-done(((f32[3,3,128,128]{3,2,1,0:T(8,128)}, f32[2,2,128,256]{3,2,1,0:T(8,128)}, f32[3,3,256,256]{3,2,1,0:T(8,128)}), (f32[3,3,128,128]{3,2,1,0:T(8,128)}, f32[2,2,128,256]{3,2,1,0:T(8,128)}, f32[3,3,256,256]{3,2,1,0:T(8,128)})) %all-reduce.3.cloned.1.call-update) | async-done | bytes 3473424 | tf_op jit(solution)/shard_map/psum | solution.py:127
  606.4 1.9 multiply_convert_fusion.1
  609.1 2.9 multiply_convert_fusion
  (208 shorter events, 38.4 us)
Async XLA Ops:
  7.2 29.1 %copy-start = (bf16[2,2,128,256]{3,2,1,0:T(8,128)(2,1)S(1)}, bf16[2,2,128,256]{3,2,1,0:T(8,128)(2,1)}, u32[]{:S(2)}) copy-start(bf16[2,2,128,256]{3,2,1,0:T(8,128)(2,1)} %param.7) | copy-start | bytes 786436
  7.2 14.5 %copy-start.1 = (bf16[3,3,256,256]{3,2,1,0:T(8,128)(2,1)S(1)}, bf16[3,3,256,256]{3,2,1,0:T(8,128)(2,1)}, u32[]{:S(2)}) copy-start(bf16[3,3,256,256]{3,2,1,0:T(8,128)(2,1)} %param.8) | copy-start | bytes 3538948
  9.7 44.8 %all-to-all-start.1 = ((bf16[16,2,1024]{2,1,0:T(2,128)(2,1)}), bf16[16,2,1024]{2,1,0:T(2,128)(2,1)S(1)}, u32[]{:S(2)}, u32[]{:S(2)}) async-start(bf16[16,2,1024]{2,1,0:T(2,128)(2,1)} %reshape.213), calls=%async_computation.1 | async-start | bytes 131072 | tf_op jit(solution)/shard_map/all_to_all | solution.py:91
  18.9 2.8 collective-permute-start
  20.2 11.7 %copy-start.16 = (bf16[3,3,128,128]{3,2,1,0:T(8,128)(2,1)S(1)}, bf16[3,3,128,128]{3,2,1,0:T(8,128)(2,1)}, u32[]{:S(2)}) copy-start(bf16[3,3,128,128]{3,2,1,0:T(8,128)(2,1)} %param.6) | copy-start | bytes 884740
  20.2 3.6 collective-permute-start.1
  24.0 8.3 %collective-permute-start.2 = (bf16[10,1,128]{2,1,0:T(2,128)(2,1)S(1)}, bf16[10,1,128]{2,1,0:T(2,128)(2,1)S(1)}, u32[]{:S(2)}, u32[]{:S(2)}) collective-permute-start(bf16[10,1,128]{2,1,0:T(2,128)(2,1)S(1)} %get-tuple-element.27), channel_id=1, source_target_pairs={{0,1},{1,2},{2,3},{3,4},{4,5},{5,6},{6,7},{7,8},{8,9},{9,10},{10,1... | collective-permute-start | bytes 7688 | tf_op jit(solution)/shard_map/ppermute | solution.py:16
  27.4 5.9 collective-permute-start.3
  36.5 5.9 collective-permute-start.5
  37.8 4.7 collective-permute-start.4
  42.5 8.8 %collective-permute-start.6 = (bf16[6,1,256]{2,1,0:T(2,128)(2,1)S(1)}, bf16[6,1,256]{2,1,0:T(2,128)(2,1)S(1)}, u32[]{:S(2)}, u32[]{:S(2)}) collective-permute-start(bf16[6,1,256]{2,1,0:T(2,128)(2,1)S(1)} %get-tuple-element.58), channel_id=1, source_target_pairs={{0,1},{1,2},{2,3},{3,4},{4,5},{5,6},{6,7},{7,8},{8,9},{9,10},{10,1... | collective-permute-start | bytes 9224 | tf_op jit(solution)/shard_map/ppermute | solution.py:16
  45.2 6.6 %collective-permute-start.7 = (bf16[6,1,256]{2,1,0:T(2,128)(2,1)S(1)}, bf16[6,1,256]{2,1,0:T(2,128)(2,1)S(1)}, u32[]{:S(2)}, u32[]{:S(2)}) collective-permute-start(bf16[6,1,256]{2,1,0:T(2,128)(2,1)S(1)} %get-tuple-element.59), channel_id=1, source_target_pairs={{1,0},{2,1},{3,2},{4,3},{5,4},{6,5},{7,6},{8,7},{9,8},{10,9},{11,1... | collective-permute-start | bytes 9224 | tf_op jit(solution)/shard_map/ppermute | solution.py:18
  63.2 14.1 %copy-start.42 = (bf16[1,32,256]{2,1,0:T(8,128)(2,1)S(1)}, bf16[1,32,256]{2,1,0:T(8,128)(2,1)}, u32[]{:S(2)}) copy-start(bf16[1,32,256]{2,1,0:T(8,128)(2,1)} %get-tuple-element.63) | copy-start | bytes 49156
  68.8 12.9 %copy-start.17 = (f32[1,256,256]{2,1,0:T(8,128)S(1)}, f32[1,256,256]{2,1,0:T(8,128)}, u32[]{:S(2)}) copy-start(f32[1,256,256]{2,1,0:T(8,128)} %convolution_bitcast_fusion.6) | copy-start | bytes 786436
  68.8 49.9 %all-to-all-start = ((bf16[16,2,1024]{2,1,0:T(2,128)(2,1)}), bf16[16,2,1024]{2,1,0:T(2,128)(2,1)S(1)}, u32[]{:S(2)}, u32[]{:S(2)}) async-start(bf16[16,2,1024]{2,1,0:T(2,128)(2,1)} %reshape.211), calls=%async_computation | async-start | bytes 131072 | tf_op jit(solution)/shard_map/all_to_all | solution.py:90
  77.3 529.1 %all-reduce.3.cloned.1.call-start = ((), (), s32[]{:S(2)}) async-start(), calls=%async_computation.2 | async-start | bytes 6946816 | tf_op jit(solution)/shard_map/psum | solution.py:127
  77.3 7.1 %collective-permute-start.9 = (bf16[1,32,256]{2,1,0:T(8,128)(2,1)S(1)}, bf16[1,32,256]{2,1,0:T(8,128)(2,1)S(1)}, u32[]{:S(2)}, u32[]{:S(2)}) collective-permute-start(bf16[1,32,256]{2,1,0:T(8,128)(2,1)S(1)} %copy-done.42), channel_id=1, source_target_pairs={{16,0},{32,16},{48,32},{64,48},{80,64},{96,80},{112,96},{128,112},... | collective-permute-start | bytes 49160 | tf_op jit(solution)/shard_map/ppermute | solution.py:18
  78.7 5.8 collective-permute-start.8
  84.5 8.2 %collective-permute-start.10 = (bf16[6,1,256]{2,1,0:T(2,128)(2,1)S(1)}, bf16[6,1,256]{2,1,0:T(2,128)(2,1)S(1)}, u32[]{:S(2)}, u32[]{:S(2)}) collective-permute-start(bf16[6,1,256]{2,1,0:T(2,128)(2,1)S(1)} %get-tuple-element.54), channel_id=1, source_target_pairs={{0,1},{1,2},{2,3},{3,4},{4,5},{5,6},{6,7},{7,8},{8,9},{9,10},{10,1... | collective-permute-start | bytes 9224 | tf_op jit(solution)/shard_map/ppermute | solution.py:16
  87.9 5.9 collective-permute-start.11
  98.4 8.4 %collective-permute-start.13 = (bf16[1,64,128]{2,1,0:T(8,128)(2,1)S(1)}, bf16[1,64,128]{2,1,0:T(8,128)(2,1)S(1)}, u32[]{:S(2)}, u32[]{:S(2)}) collective-permute-start(bf16[1,64,128]{2,1,0:T(8,128)(2,1)S(1)} %get-tuple-element.32), channel_id=1, source_target_pairs={{16,0},{32,16},{48,32},{64,48},{80,64},{96,80},{112,96},{128,112},... | collective-permute-start | bytes 49160 | tf_op jit(solution)/shard_map/ppermute | solution.py:18
  99.7 7.1 %collective-permute-start.12 = (bf16[1,64,128]{2,1,0:T(8,128)(2,1)S(1)}, bf16[1,64,128]{2,1,0:T(8,128)(2,1)S(1)}, u32[]{:S(2)}, u32[]{:S(2)}) collective-permute-start(bf16[1,64,128]{2,1,0:T(8,128)(2,1)S(1)} %get-tuple-element.31), channel_id=1, source_target_pairs={{0,16},{16,32},{32,48},{48,64},{64,80},{80,96},{96,112},{112,128},... | collective-permute-start | bytes 49160 | tf_op jit(solution)/shard_map/ppermute | solution.py:16
  106.9 8.3 %collective-permute-start.14 = (bf16[10,1,128]{2,1,0:T(2,128)(2,1)S(1)}, bf16[10,1,128]{2,1,0:T(2,128)(2,1)S(1)}, u32[]{:S(2)}, u32[]{:S(2)}) collective-permute-start(bf16[10,1,128]{2,1,0:T(2,128)(2,1)S(1)} %get-tuple-element.22), channel_id=1, source_target_pairs={{0,1},{1,2},{2,3},{3,4},{4,5},{5,6},{6,7},{7,8},{8,9},{9,10},{10,1... | collective-permute-start | bytes 7688 | tf_op jit(solution)/shard_map/ppermute | solution.py:16
  109.7 6.6 %collective-permute-start.15 = (bf16[10,1,128]{2,1,0:T(2,128)(2,1)S(1)}, bf16[10,1,128]{2,1,0:T(2,128)(2,1)S(1)}, u32[]{:S(2)}, u32[]{:S(2)}) collective-permute-start(bf16[10,1,128]{2,1,0:T(2,128)(2,1)S(1)} %get-tuple-element.23), channel_id=1, source_target_pairs={{1,0},{2,1},{3,2},{4,3},{5,4},{6,5},{7,6},{8,7},{9,8},{10,9},{11,1... | collective-permute-start | bytes 7688 | tf_op jit(solution)/shard_map/ppermute | solution.py:18
  (38 other events, 90.3 us)
Sparse Core Ops, SparseCore 0:
  106.9 499.4 all-reduce.2
where the time goes:
time: 620 us; the launch traced here: 619 us
  waiting for transfers between devices  492 us (79%)
  starting transfers between devices  68.3 us (11%)
  matrix products  19 us (3%)
  between operations  15.2 us (2%)
  local copies, waits for them, and re-layouts  15 us (2%)
  other arithmetic  9.4 us (2%)
    psum x1, waiting for transfers between devices, local(): reduced = lax.psum((level_wgrad, down_wgrad, neck_wgrad), ('gy', 'gx'))  487 us
    ppermute x8, starting transfers between devices, extended(): lax.ppermute(tail, axis, [(i, (i + 1) % count) for i in range(ends)])  25.5 us
    ppermute x8, starting transfers between devices, extended(): lax.ppermute(head, axis, [((i + 1) % count, i) for i in range(ends)])  25 us
  transfers between devices with their start and end apart: 19, of which 7 were waited for; matrix products, arithmetic and copies ran while one was open for 3% of the time, Pallas kernels for 0%

commit v1 on v0

--- a/solution.py
+++ b/solution.py
@@ -124,7 +124,7 @@
     level_count = tile_rows * tile_cols * device_count
     level_scale = 1.0 / math.sqrt(level_count)
     neck_scale = 1.0 / math.sqrt(level_count // 4)
-    reduced = lax.psum((level_wgrad, down_wgrad, neck_wgrad), ("gy", "gx"))
+    reduced = lax.psum(lax.psum((level_wgrad, down_wgrad, neck_wgrad), "gx"), "gy")
     grad_level = (reduced[0] * level_scale).astype(jnp.bfloat16)
     grad_down = (reduced[1] * neck_scale).astype(jnp.bfloat16)
     grad_neck = (reduced[2] * neck_scale).astype(jnp.bfloat16)

time: 620 us -> 460 us (0.74)
  the two profiles are of different devices: /device:TPU:2 before, /device:TPU:1 now
where the time goes in v1:
time: 460 us; the launch traced here: 459 us
  waiting for transfers between devices  348 us (76%)
  starting transfers between devices  60.5 us (13%)
  matrix products  15.6 us (3%)
  between operations  15.3 us (3%)
  local copies, waits for them, and re-layouts  10.8 us (2%)
  other arithmetic  9.43 us (2%)
    psum x1, waiting for transfers between devices, local(): lax.psum(lax.psum((level_wgrad, down_wgrad, neck_wgrad), 'gx'), 'gy')  217 us
    psum x1, waiting for transfers between devices, local(): lax.psum((level_wgrad, down_wgrad, neck_wgrad), 'gx')  115 us
    ppermute x8, starting transfers between devices, extended(): lax.ppermute(tail, axis, [(i, (i + 1) % count) for i in range(ends)])  32.5 us
    ppermute x8, waiting for transfers between devices, extended(): lax.ppermute(head, axis, [((i + 1) % count, i) for i in range(ends)])  14.3 us
    ppermute x8, starting transfers between devices, extended(): lax.ppermute(head, axis, [((i + 1) % count, i) for i in range(ends)])  13.1 us
    dot_general x36, matrix products, conv_padded(): jnp.dot(window, weights[offset_y, offset_x], preferred_element_type=jnp.f...  10.3 us
  transfers between devices with their start and end apart: 20, of which 8 were waited for; matrix products, arithmetic and copies ran while one was open for 3% of the time, Pallas kernels for 0%

profile of v1, /device:TPU:1, one launch (start us, length us, event | category | flops | bytes accessed | tf_op | source)
XLA Modules:
  0.0 459.3 jit_solution(10485052559811039487)
XLA Ops:
  8.0 4.9 %collective-permute-start = (bf16[1,64,128]{2,1,0:T(8,128)(2,1)S(1)}, bf16[1,64,128]{2,1,0:T(8,128)(2,1)S(1)}, u32[]{:S(2)}, u32[]{:S(2)}) collective-permute-start(bf16[1,64,128]{2,1,0:T(8,128)(2,1)S(1)} %get-tuple-element.42), channel_id=1, source_target_pairs={{0,16},{16,32},{32,48},{48,64},{64,80},{80,96},{96,112},{112,128},... | collective-permute-start | bytes 49160 | tf_op jit(solution)/shard_map/ppermute | solution.py:16
  15.3 6.8 %all-to-all-start.1 = ((bf16[16,2,1024]{2,1,0:T(2,128)(2,1)}), bf16[16,2,1024]{2,1,0:T(2,128)(2,1)S(1)}, u32[]{:S(2)}, u32[]{:S(2)}) async-start(bf16[16,2,1024]{2,1,0:T(2,128)(2,1)} %reshape.213), calls=%async_computation.1 | async-start | bytes 131072 | tf_op jit(solution)/shard_map/all_to_all | solution.py:91
  22.1 1.9 collective-permute-start.1
  24.1 3.4 collective-permute-done.1
  27.6 3.3 collective-permute-start.2
  32.5 2.7 collective-permute-done.3
  37.8 1.9 collective-permute-start.5
  39.7 3.6 collective-permute-start.4
  44.2 3.1 collective-permute-start.6
  49.4 2.3 collective-permute-done.7
  62.3 2.1 collective-permute-start.9
  64.4 5.5 %collective-permute-start.8 = (bf16[1,32,256]{2,1,0:T(8,128)(2,1)S(1)}, bf16[1,32,256]{2,1,0:T(8,128)(2,1)S(1)}, u32[]{:S(2)}, u32[]{:S(2)}) collective-permute-start(bf16[1,32,256]{2,1,0:T(8,128)(2,1)S(1)} %get-tuple-element.65), channel_id=1, source_target_pairs={{0,16},{16,32},{32,48},{48,64},{64,80},{80,96},{96,112},{112,128},... | collective-permute-start | bytes 49160 | tf_op jit(solution)/shard_map/ppermute | solution.py:16
  70.0 1.6 pad_maximum_fusion
  71.6 4.3 collective-permute-start.10
  77.5 3.1 collective-permute-done.11
  87.3 2.1 collective-permute-start.13
  89.4 4.5 collective-permute-start.12
  95.0 8.1 %all-to-all-start = ((bf16[16,2,1024]{2,1,0:T(2,128)(2,1)}), bf16[16,2,1024]{2,1,0:T(2,128)(2,1)S(1)}, u32[]{:S(2)}, u32[]{:S(2)}) async-start(bf16[16,2,1024]{2,1,0:T(2,128)(2,1)} %reshape.211), calls=%async_computation | async-start | bytes 131072 | tf_op jit(solution)/shard_map/all_to_all | solution.py:90
  103.1 3.3 collective-permute-start.14
  107.9 2.8 collective-permute-done.15
  111.0 115.4 %all-reduce.7.cloned.1.call-done = (f32[3,3,128,128]{3,2,1,0:T(8,128)}, f32[2,2,128,256]{3,2,1,0:T(8,128)}, f32[3,3,256,256]{3,2,1,0:T(8,128)}) async-done(((f32[3,3,128,128]{3,2,1,0:T(8,128)}, f32[2,2,128,256]{3,2,1,0:T(8,128)}, f32[3,3,256,256]{3,2,1,0:T(8,128)}), (f32[3,3,128,128]{3,2,1,0:T(8,128)}, f32[2,2,128,256]{3,2,1,0:T(8,128)}, f32[3,3,256,256]{3,2,1,0:T(8,128)})) %all-reduce.7.cloned.1.call-update) | async-done | bytes 3473424 | tf_op jit(solution)/shard_map/psum | solution.py:127
  229.9 217.0 %all-reduce.5.cloned.1.call-done = (f32[3,3,128,128]{3,2,1,0:T(8,128)}, f32[2,2,128,256]{3,2,1,0:T(8,128)}, f32[3,3,256,256]{3,2,1,0:T(8,128)}) async-done(((f32[3,3,128,128]{3,2,1,0:T(8,128)}, f32[2,2,128,256]{3,2,1,0:T(8,128)}, f32[3,3,256,256]{3,2,1,0:T(8,128)}), (f32[3,3,128,128]{3,2,1,0:T(8,128)}, f32[2,2,128,256]{3,2,1,0:T(8,128)}, f32[3,3,256,256]{3,2,1,0:T(8,128)})) %all-reduce.5.cloned.1.call-update) | async-done | bytes 3473424 | tf_op jit(solution)/shard_map/psum | solution.py:127
  446.9 1.9 multiply_convert_fusion.1
  449.5 2.9 multiply_convert_fusion
  (201 shorter events, 35.5 us)
Async XLA Ops:
  7.2 30.4 %copy-start = (bf16[2,2,128,256]{3,2,1,0:T(8,128)(2,1)S(1)}, bf16[2,2,128,256]{3,2,1,0:T(8,128)(2,1)}, u32[]{:S(2)}) copy-start(bf16[2,2,128,256]{3,2,1,0:T(8,128)(2,1)} %param.7) | copy-start | bytes 786436
  7.2 20.3 %copy-start.2 = (bf16[8,64,128]{2,1,0:T(8,128)(2,1)S(1)}, bf16[8,64,128]{2,1,0:T(8,128)(2,1)}, u32[]{:S(2)}) copy-start(bf16[8,64,128]{2,1,0:T(8,128)(2,1)} %param.5) | copy-start | bytes 393220
  7.2 25.0 %copy-start.15 = (bf16[3,3,128,128]{3,2,1,0:T(8,128)(2,1)S(1)}, bf16[3,3,128,128]{3,2,1,0:T(8,128)(2,1)}, u32[]{:S(2)}) copy-start(bf16[3,3,128,128]{3,2,1,0:T(8,128)(2,1)} %param.6) | copy-start | bytes 884740
  8.0 16.0 %collective-permute-start = (bf16[1,64,128]{2,1,0:T(8,128)(2,1)S(1)}, bf16[1,64,128]{2,1,0:T(8,128)(2,1)S(1)}, u32[]{:S(2)}, u32[]{:S(2)}) collective-permute-start(bf16[1,64,128]{2,1,0:T(8,128)(2,1)S(1)} %get-tuple-element.42), channel_id=1, source_target_pairs={{0,16},{16,32},{32,48},{48,64},{64,80},{80,96},{96,112},{112,128},... | collective-permute-start | bytes 49160 | tf_op jit(solution)/shard_map/ppermute | solution.py:16
  15.3 39.1 %all-to-all-start.1 = ((bf16[16,2,1024]{2,1,0:T(2,128)(2,1)}), bf16[16,2,1024]{2,1,0:T(2,128)(2,1)S(1)}, u32[]{:S(2)}, u32[]{:S(2)}) async-start(bf16[16,2,1024]{2,1,0:T(2,128)(2,1)} %reshape.213), calls=%async_computation.1 | async-start | bytes 131072 | tf_op jit(solution)/shard_map/all_to_all | solution.py:91
  22.1 204.4 %all-reduce.7.cloned.1.call-start = ((), (), s32[]{:S(2)}) async-start(), calls=%async_computation.3 | async-start | bytes 6946816 | tf_op jit(solution)/shard_map/psum | solution.py:127
  22.1 5.4 %collective-permute-start.1 = (bf16[1,64,128]{2,1,0:T(8,128)(2,1)S(1)}, bf16[1,64,128]{2,1,0:T(8,128)(2,1)S(1)}, u32[]{:S(2)}, u32[]{:S(2)}) collective-permute-start(bf16[1,64,128]{2,1,0:T(8,128)(2,1)S(1)} %get-tuple-element.41), channel_id=1, source_target_pairs={{16,0},{32,16},{48,32},{64,48},{80,64},{96,80},{112,96},{128,112},... | collective-permute-start | bytes 49160 | tf_op jit(solution)/shard_map/ppermute | solution.py:18
  27.6 4.9 %collective-permute-start.2 = (bf16[10,1,128]{2,1,0:T(2,128)(2,1)S(1)}, bf16[10,1,128]{2,1,0:T(2,128)(2,1)S(1)}, u32[]{:S(2)}, u32[]{:S(2)}) collective-permute-start(bf16[10,1,128]{2,1,0:T(2,128)(2,1)S(1)} %get-tuple-element.30), channel_id=1, source_target_pairs={{0,1},{1,2},{2,3},{3,4},{4,5},{5,6},{6,7},{7,8},{8,9},{9,10},{10,1... | collective-permute-start | bytes 7688 | tf_op jit(solution)/shard_map/ppermute | solution.py:16
  30.9 4.4 collective-permute-start.3
  36.6 6.8 %copy-start.1 = (bf16[3,3,256,256]{3,2,1,0:T(8,128)(2,1)S(1)}, bf16[3,3,256,256]{3,2,1,0:T(8,128)(2,1)}, u32[]{:S(2)}) copy-start(bf16[3,3,256,256]{3,2,1,0:T(8,128)(2,1)} %param.8) | copy-start | bytes 3538948
  37.8 5.7 %collective-permute-start.5 = (bf16[1,32,256]{2,1,0:T(8,128)(2,1)S(1)}, bf16[1,32,256]{2,1,0:T(8,128)(2,1)S(1)}, u32[]{:S(2)}, u32[]{:S(2)}) collective-permute-start(bf16[1,32,256]{2,1,0:T(8,128)(2,1)S(1)} %get-tuple-element.70), channel_id=1, source_target_pairs={{16,0},{32,16},{48,32},{64,48},{80,64},{96,80},{112,96},{128,112},... | collective-permute-start | bytes 49160 | tf_op jit(solution)/shard_map/ppermute | solution.py:18
  39.7 4.5 collective-permute-start.4
  44.2 5.2 %collective-permute-start.6 = (bf16[6,1,256]{2,1,0:T(2,128)(2,1)S(1)}, bf16[6,1,256]{2,1,0:T(2,128)(2,1)S(1)}, u32[]{:S(2)}, u32[]{:S(2)}) collective-permute-start(bf16[6,1,256]{2,1,0:T(2,128)(2,1)S(1)} %get-tuple-element.61), channel_id=1, source_target_pairs={{0,1},{1,2},{2,3},{3,4},{4,5},{5,6},{6,7},{7,8},{8,9},{9,10},{10,1... | collective-permute-start | bytes 9224 | tf_op jit(solution)/shard_map/ppermute | solution.py:16
  47.3 4.4 collective-permute-start.7
  62.3 9.3 %collective-permute-start.9 = (bf16[1,32,256]{2,1,0:T(8,128)(2,1)S(1)}, bf16[1,32,256]{2,1,0:T(8,128)(2,1)S(1)}, u32[]{:S(2)}, u32[]{:S(2)}) collective-permute-start(bf16[1,32,256]{2,1,0:T(8,128)(2,1)S(1)} %get-tuple-element.66), channel_id=1, source_target_pairs={{16,0},{32,16},{48,32},{64,48},{80,64},{96,80},{112,96},{128,112},... | collective-permute-start | bytes 49160 | tf_op jit(solution)/shard_map/ppermute | solution.py:18
  64.4 7.2 %collective-permute-start.8 = (bf16[1,32,256]{2,1,0:T(8,128)(2,1)S(1)}, bf16[1,32,256]{2,1,0:T(8,128)(2,1)S(1)}, u32[]{:S(2)}, u32[]{:S(2)}) collective-permute-start(bf16[1,32,256]{2,1,0:T(8,128)(2,1)S(1)} %get-tuple-element.65), channel_id=1, source_target_pairs={{0,16},{16,32},{32,48},{48,64},{64,80},{80,96},{96,112},{112,128},... | collective-permute-start | bytes 49160 | tf_op jit(solution)/shard_map/ppermute | solution.py:16
  71.6 5.9 %collective-permute-start.10 = (bf16[6,1,256]{2,1,0:T(2,128)(2,1)S(1)}, bf16[6,1,256]{2,1,0:T(2,128)(2,1)S(1)}, u32[]{:S(2)}, u32[]{:S(2)}) collective-permute-start(bf16[6,1,256]{2,1,0:T(2,128)(2,1)S(1)} %get-tuple-element.57), channel_id=1, source_target_pairs={{0,1},{1,2},{2,3},{3,4},{4,5},{5,6},{6,7},{7,8},{8,9},{9,10},{10,1... | collective-permute-start | bytes 9224 | tf_op jit(solution)/shard_map/ppermute | solution.py:16
  76.0 4.7 %collective-permute-start.11 = (bf16[6,1,256]{2,1,0:T(2,128)(2,1)S(1)}, bf16[6,1,256]{2,1,0:T(2,128)(2,1)S(1)}, u32[]{:S(2)}, u32[]{:S(2)}) collective-permute-start(bf16[6,1,256]{2,1,0:T(2,128)(2,1)S(1)} %get-tuple-element.58), channel_id=1, source_target_pairs={{1,0},{2,1},{3,2},{4,3},{5,4},{6,5},{7,6},{8,7},{9,8},{10,9},{11,1... | collective-permute-start | bytes 9224 | tf_op jit(solution)/shard_map/ppermute | solution.py:18
  87.3 15.8 %collective-permute-start.13 = (bf16[1,64,128]{2,1,0:T(8,128)(2,1)S(1)}, bf16[1,64,128]{2,1,0:T(8,128)(2,1)S(1)}, u32[]{:S(2)}, u32[]{:S(2)}) collective-permute-start(bf16[1,64,128]{2,1,0:T(8,128)(2,1)S(1)} %get-tuple-element.35), channel_id=1, source_target_pairs={{16,0},{32,16},{48,32},{64,48},{80,64},{96,80},{112,96},{128,112},... | collective-permute-start | bytes 49160 | tf_op jit(solution)/shard_map/ppermute | solution.py:18
  89.4 13.8 %collective-permute-start.12 = (bf16[1,64,128]{2,1,0:T(8,128)(2,1)S(1)}, bf16[1,64,128]{2,1,0:T(8,128)(2,1)S(1)}, u32[]{:S(2)}, u32[]{:S(2)}) collective-permute-start(bf16[1,64,128]{2,1,0:T(8,128)(2,1)S(1)} %get-tuple-element.34), channel_id=1, source_target_pairs={{0,16},{16,32},{32,48},{48,64},{64,80},{80,96},{96,112},{112,128},... | collective-permute-start | bytes 49160 | tf_op jit(solution)/shard_map/ppermute | solution.py:16
  95.0 133.7 %all-to-all-start = ((bf16[16,2,1024]{2,1,0:T(2,128)(2,1)}), bf16[16,2,1024]{2,1,0:T(2,128)(2,1)S(1)}, u32[]{:S(2)}, u32[]{:S(2)}) async-start(bf16[16,2,1024]{2,1,0:T(2,128)(2,1)} %reshape.211), calls=%async_computation | async-start | bytes 131072 | tf_op jit(solution)/shard_map/all_to_all | solution.py:90
  103.1 343.8 %all-reduce.5.cloned.1.call-start = ((), (), s32[]{:S(2)}) async-start(), calls=%async_computation.2 | async-start | bytes 6946816 | tf_op jit(solution)/shard_map/psum | solution.py:127
  103.1 4.8 %collective-permute-start.14 = (bf16[10,1,128]{2,1,0:T(2,128)(2,1)S(1)}, bf16[10,1,128]{2,1,0:T(2,128)(2,1)S(1)}, u32[]{:S(2)}, u32[]{:S(2)}) collective-permute-start(bf16[10,1,128]{2,1,0:T(2,128)(2,1)S(1)} %get-tuple-element.25), channel_id=1, source_target_pairs={{0,1},{1,2},{2,3},{3,4},{4,5},{5,6},{6,7},{7,8},{8,9},{9,10},{10,1... | collective-permute-start | bytes 7688 | tf_op jit(solution)/shard_map/ppermute | solution.py:16
  106.4 4.4 collective-permute-start.15
  (34 other events, 59.3 us)
Sparse Core Ops, SparseCore 0:
  87.4 138.9 all-reduce.6
  229.2 217.6 all-reduce.4
